TPU v7x, 128 devices: a whole 4x4x4 slice. The times are simulated.
128 devices in a mesh: dp: 32 (over x, y, core), tensor: 4 (over z).
Axes of the slice: x: 4, y: 4, z: 4, core: 2. Of those that a mesh axis runs over, the one named last changes fastest.
Arguments:
- activations: bfloat16 [32, 1536, 2048], P('dp', 'tensor'), may hold values from -6 to 6
- upstream_grad: bfloat16 [32, 1536, 4096], P('dp', None, 'tensor'), may hold values from -0.15625 to 0.15625
- feedback: bfloat16 [32, 2048, 4096], P('dp', None, 'tensor'), may hold values from -3 to 3
- selected: int32 [32, 4, 2], P('dp', 'tensor'), may hold values from -1 to 255, as said below
- cycle_values: bfloat16 [8, 4, 64, 64, 128], P(None, 'tensor'), may hold values from -6 to 6
- cycle_blocks: int32 [8, 4, 64], P(None, 'tensor'), may hold values from -1 to 255, as said below
- cycle_position: int32 [1], replicated, may hold values from 0 to 7
Outputs:
- update_dir: bfloat16 [2048, 4096], P(None, 'tensor')
- new_feedback: bfloat16 [32, 2048, 4096], P('dp', None, 'tensor')
- newest_values: bfloat16 [4, 64, 64, 128], P('tensor')
Inputs may be any that keep to these rules, and one draw needn't show every extreme that they name: `selected`: for each replica and tensor shard, the 2 entries hold 1 to 2 distinct block numbers first, then -1; in every tensor shard some replica lists 2 blocks. `cycle_blocks`: within each slot and tensor shard, entries r * 2 to r * 2 + 1 hold 1 to 2 distinct block numbers first, then -1; in every slot and shard some group of 2 entries is full.
All inputs are finite; a program needn't handle non-finite values.
Results may differ from a plain program's by a relative error of at most 0.0023.
Values may be sent and summed in bfloat16 or wider, within the bound.
No kernel may reach another device: no remote copies, remote signals or barrier semaphores. Data moves between devices by JAX's collectives and lax.ppermute only.
A program may use at most 192 MiB of HBM per device.

v0:
```python
import jax
import jax.numpy as jnp
from jax import lax
from jax.sharding import PartitionSpec as P

D = 2048
BH = 64
BW = 128
SLOTS = 8
decay_first = 0.9
decay_second = 0.999
epsilon = 0.001


def to_blocks(matrix):
    row_blocks = matrix.shape[0] // BH
    col_blocks = matrix.shape[1] // BW
    return (
        matrix.reshape(row_blocks, BH, col_blocks, BW)
        .transpose(0, 2, 1, 3)
        .reshape(row_blocks * col_blocks, BH, BW)
    )


def from_blocks(blocks, height, breadth):
    return (
        blocks.reshape(height // BH, breadth // BW, BH, BW)
        .transpose(0, 2, 1, 3)
        .reshape(height, breadth)
    )


def local(
    activations, upstream_grad, feedback, selected, cycle_values, cycle_blocks, cycle_position
):
    token_rows = activations[0]
    upstream = upstream_grad[0]
    shard_width = upstream.shape[1]
    contract = (((0,), (0,)), ((), ()))
    gathered = lax.all_gather(token_rows, "tensor", axis=0, tiled=True)
    gradient = lax.dot_general(gathered, upstream, contract, preferred_element_type=jnp.float32)
    accumulated = gradient + feedback[0].astype(jnp.float32)
    blocks = to_blocks(accumulated)
    block_total = blocks.shape[0]
    chosen = selected[0, 0]
    is_live = chosen >= 0
    safe_index = jnp.where(is_live, chosen, 0)
    outgoing = (blocks[safe_index] * is_live[:, None, None]).astype(jnp.bfloat16)
    cleared = jnp.any(jnp.arange(block_total)[:, None] == chosen[None, :], axis=1)
    remaining = jnp.where(cleared[:, None, None], 0.0, blocks)
    new_feedback = from_blocks(remaining, D, shard_width).astype(jnp.bfloat16)[None]
    all_values, all_blocks = (
        lax.all_gather(outgoing, "dp", axis=0, tiled=True),
        lax.all_gather(chosen, "dp", axis=0, tiled=True),
    )
    entry_total = all_values.shape[0]
    position = cycle_position[0]
    targets = jnp.arange(block_total)
    first_moment = jnp.zeros((block_total, BH * BW), jnp.float32)
    second_moment = jnp.zeros((block_total, BH * BW), jnp.float32)
    for slot_number in range(SLOTS):
        newest = position == slot_number
        values = jnp.where(newest, all_values, cycle_values[slot_number, 0])
        listed = jnp.where(newest, all_blocks, cycle_blocks[slot_number, 0])
        onehot = (targets[:, None] == listed[None, :]).astype(jnp.bfloat16)
        densified = jnp.dot(
            onehot, values.reshape(entry_total, BH * BW), preferred_element_type=jnp.float32
        )
        slot_age = jnp.mod(position - slot_number, SLOTS).astype(jnp.float32)
        weight_first = (1.0 - decay_first) * jnp.power(decay_first, slot_age)
        weight_second = (1.0 - decay_second) * jnp.power(decay_second, slot_age)
        first_moment = first_moment + weight_first * densified
        second_moment = second_moment + weight_second * (densified * densified)
    update = (
        (first_moment / (jnp.sqrt(second_moment) + epsilon))
        .astype(jnp.bfloat16)
        .reshape(block_total, BH, BW)
    )
    update_dir = from_blocks(update, D, shard_width)
    return (update_dir, new_feedback, all_values[None])


def solution(mesh):
    placed = (
        P("dp", "tensor", None),
        P("dp", None, "tensor"),
        P("dp", None, "tensor"),
        P("dp", "tensor", None),
        P(None, "tensor", None, None, None),
        P(None, "tensor", None),
        P(),
    )
    return jax.shard_map(
        local,
        mesh=mesh,
        in_specs=placed,
        out_specs=(P(None, "tensor"), P("dp", None, "tensor"), P("tensor", None, None, None)),
        check_vma=False,
    )
```

profile of v0, /device:TPU:1, one launch (start us, length us, event | category | flops | bytes accessed | tf_op | source)
XLA Modules:
  0.0 211.0 jit_solution(4553705174519842768)
XLA Ops:
  7.2 0.0 copy-start
  7.2 0.0 all-gather.7.cloned.1.call-start
  7.2 0.7 all-gather.7.cloned.1.call-update
  7.9 0.0 all-gather.5.cloned.1.call-start
  8.0 0.9 compare_reduce_fusion
  8.9 0.1 broadcast_in_dim.20
  9.0 0.7 fusion.44
  9.6 0.7 compare_convert_fusion
  10.3 68.5 %all-gather.7.cloned.1.call-done = bf16[1,1536,2048]{2,1,0:T(8,128)(2,1)} async-done(((bf16[1,384,2048]{2,1,0:T(8,128)(2,1)}), bf16[1,1536,2048]{2,1,0:T(8,128)(2,1)}) %all-gather.7.cloned.1.call-update) | async-done | bytes 6291472 | tf_op jit(solution)/shard_map/all_gather | solution.py:40
  78.8 0.6 broadcast_in_dim.21
  79.4 12.2 %fusion.3 = (bf16[1,2048,1024]{2,1,0:T(8,128)(2,1)}, f32[256,8,8,128]{3,1,2,0:T(8,128)S(1)}) fusion(pred[256,8,8,128]{3,2,1,0:T(8,128)(4,1)S(1)} %bitcast.150, bf16[1,2048,1024]{2,1,0:T(8,128)(2,1)} %param.9, bf16[1,1536,1024]{2,1,0:T(8,128)(2,1)S(1)} %copy-done, bf16[1,1536,2048]{2,1,0:T(8,128)(2,1)} %all-gather.7.cloned.1.call-done), kind=kOutput, calls=%fused_computation.7 | convolution fusion | flops 6450839552 | bytes 28311552 | tf_op jit(solution)/shard_map/dot_general | solution.py:41
  91.6 2.1 copy.13
  93.7 0.0 copy-start.5
  93.8 4.9 %copy.12 = f32[32,64,8,128]{3,1,2,0:T(8,128)} copy(f32[32,64,8,128]{3,2,1,0:T(8,128)S(1)} %bitcast.138) | data formatting | bytes 16777216 | tf_op jit(solution)/shard_map/reshape | solution.py:19
  98.6 3.9 %gather_fusion = f32[2,64,128]{2,1,0:T(8,128)S(1)} fusion(f32[256,64,128]{2,1,0:T(8,128)} %bitcast.139, s32[1024]{0:T(1024)S(1)} %pad_clamp_fusion), kind=kCustom, calls=%fused_computation | custom fusion | bytes 131080 | tf_op jit(solution)/shard_map/gather | solution.py:48
  102.6 0.7 multiply_convert_fusion
  103.3 0.0 all-gather.5.cloned.1.call-update
  104.7 0.6 dynamic-slice
  106.0 0.1 bitcast_dynamic-update-slice_fusion
  106.1 13.3 %all-reduce = s32[64]{0:T(128)S(1)} all-reduce(s32[64]{0:T(128)S(1)} %bitcast_dynamic-update-slice_fusion), channel_id=2, replica_groups=mesh['dp'=32,'tensor'=4] {'dp'}, use_global_device_ids=true, to_apply=%add | all-reduce | flops 64 | bytes 512
  119.4 27.6 %all-gather.5.cloned.1.call-done = bf16[64,64,128]{2,1,0:T(8,128)(2,1)} async-done(((bf16[2,64,128]{2,1,0:T(8,128)(2,1)}), bf16[64,64,128]{2,1,0:T(8,128)(2,1)}) %all-gather.5.cloned.1.call-update) | async-done | bytes 1048592 | tf_op jit(solution)/shard_map/all_gather | solution.py:53
  147.0 4.0 %bitcast_select_fusion = (bf16[64,64,128]{2,1,0:T(8,128)(2,1)S(1)}, bf16[64,64,128]{2,1,0:T(8,128)(2,1)S(1)}, bf16[64,64,128]{2,1,0:T(8,128)(2,1)S(1)}, bf16[64,...) fusion(bf16[64,64,128]{2,1,0:T(8,128)(2,1)} %all-gather.5.clone, ...), kind=kLoop, calls=%fused_computation.33 | loop fusion | flops 4194304 | bytes 17825800 | tf_op jit(solution)/shard_map/jit(_where)/select_n | solution.py:63
  151.1 1.3 fusion.7
  152.3 1.3 fusion.10
  153.6 4.5 %fusion.13 = f32[256,8192]{1,0:T(8,128)} fusion(bf16[8,8,64,128]{3,2,1,0:T(8,128)(2,1)S(1)} %bitcast.144, s32[64]{0:T(128)S(1)} %get-tuple-element.18), kind=kOutput, calls=%fused_computation.18 | convolution fusion | flops 268451840 | bytes 9437440 | tf_op jit(solution)/shard_map/dot_general | solution.py:66
  158.2 4.5 %fusion.16 = f32[256,8192]{1,0:T(8,128)} fusion(bf16[8,8,64,128]{3,2,1,0:T(8,128)(2,1)S(1)} %bitcast.143, s32[64]{0:T(128)S(1)} %get-tuple-element.17), kind=kOutput, calls=%fused_computation.21 | convolution fusion | flops 268451840 | bytes 9437440 | tf_op jit(solution)/shard_map/dot_general | solution.py:66
  162.7 4.5 %fusion.19 = f32[256,8192]{1,0:T(8,128)} fusion(bf16[8,8,64,128]{3,2,1,0:T(8,128)(2,1)S(1)} %bitcast.142, s32[64]{0:T(128)S(1)} %get-tuple-element.16), kind=kOutput, calls=%fused_computation.24 | convolution fusion | flops 268451840 | bytes 9437440 | tf_op jit(solution)/shard_map/dot_general | solution.py:66
  167.2 4.5 %fusion.22 = f32[256,8192]{1,0:T(8,128)} fusion(bf16[8,8,64,128]{3,2,1,0:T(8,128)(2,1)S(1)} %bitcast.141, s32[64]{0:T(128)S(1)} %get-tuple-element.15), kind=kOutput, calls=%fused_computation.27 | convolution fusion | flops 268451840 | bytes 9437440 | tf_op jit(solution)/shard_map/dot_general | solution.py:66
  171.7 4.5 %fusion.25 = f32[256,8192]{1,0:T(8,128)} fusion(bf16[8,8,64,128]{3,2,1,0:T(8,128)(2,1)S(1)} %bitcast.140, s32[64]{0:T(128)S(1)} %get-tuple-element.14), kind=kOutput, calls=%fused_computation.30 | convolution fusion | flops 268451840 | bytes 9437440 | tf_op jit(solution)/shard_map/dot_general | solution.py:66
  176.2 21.6 %divide_convert_fusion = bf16[256,8192]{1,0:T(8,128)(2,1)} fusion(f32[256,8192]{1,0:T(8,128)S(1)} %fusion.7, f32[256,8192]{1,0:T(8,128)S(1)} %fusion.10, f32[256,8192]{1,0:T(8,128)} %fusion.13, f32[256,8192]{1,0:T(8,128)} %fusion.16, f32[256,8192]{1,0:T(8,128)} %fusion.19, f32[256,8192]{1,0:T(8,128)} %fusion.22, f32[256,8192]{1,0:T(8,128)} %fusion.25, ...), kind=kOutput, calls=%fused_computation.3 | convolution fusion | flops 354435072 | bytes 63963456 | tf_op jit(solution)/shard_map/dot_general | solution.py:66
  197.8 5.4 %copy.60 = bf16[256,8,8,128]{3,1,2,0:T(8,128)(2,1)} copy(bf16[256,8,8,128]{3,2,1,0:T(8,128)(2,1)} %bitcast.148) | data formatting | bytes 8388608
  203.2 1.0 copy.64
  (13 shorter events, 0.0 us)
Async XLA Ops:
  7.2 72.3 %copy-start = (bf16[1,1536,1024]{2,1,0:T(8,128)(2,1)S(1)}, bf16[1,1536,1024]{2,1,0:T(8,128)(2,1)}, u32[]{:S(2)}) copy-start(bf16[1,1536,1024]{2,1,0:T(8,128)(2,1)} %param.8) | copy-start | bytes 9437188
  7.2 71.6 %all-gather.7.cloned.1.call-start = ((), (), s32[]{:S(2)}) async-start(), calls=%async_computation.1 | async-start | bytes 7864320 | tf_op jit(solution)/shard_map/all_gather | solution.py:40
  7.9 139.1 %all-gather.5.cloned.1.call-start = ((), (), s32[]{:S(2)}) async-start(), calls=%async_computation | async-start | bytes 1081344 | tf_op jit(solution)/shard_map/all_gather | solution.py:53
  93.7 11.0 %copy-start.5 = (u32[128]{0:T(128)S(1)}, u32[128]{0:T(128)}, u32[]{:S(2)}) copy-start(u32[128]{0:T(128)} %constant.93) | copy-start | bytes 1540
  93.7 12.3 %copy-start.4 = (s32[1,1,2]{2,1,0:T(1,128)S(1)}, s32[1,1,2]{2,1,0:T(1,128)}, u32[]{:S(2)}) copy-start(s32[1,1,2]{2,1,0:T(1,128)} %param.10) | copy-start | bytes 28
  93.8 25.7 %copy-start.3 = (s32[8,1,64]{2,1,0:T(1,128)S(1)}, s32[8,1,64]{2,1,0:T(1,128)}, u32[]{:S(2)}) copy-start(s32[8,1,64]{2,1,0:T(1,128)} %param.12) | copy-start | bytes 6148
  176.2 28.0 %copy-start.1 = (bf16[1,1536,1024]{2,1,0:T(8,128)(2,1)S(1)}, bf16[1,1536,1024]{2,1,0:T(8,128)(2,1)}, u32[]{:S(2)}) copy-start(bf16[1,1536,1024]{2,1,0:T(8,128)(2,1)} %param.8) | copy-start | bytes 9437188
  197.8 5.4 %copy-start.2 = (bf16[64,64,128]{2,1,0:T(8,128)(2,1)S(1)}, bf16[64,64,128]{2,1,0:T(8,128)(2,1)}, u32[]{:S(2)}) copy-start(bf16[64,64,128]{2,1,0:T(8,128)(2,1)} %all-gather.5.cloned.1.call-done) | copy-start | bytes 3145732
Sparse Core Ops, SparseCore 0:
  9.7 69.0 all-gather.6
  103.4 43.6 all-gather.4
where the time goes:
time: 211 us
  waiting for transfers between devices  96.8 us (46%)
  matrix products  58.9 us (28%)
  local copies, waits for them, and re-layouts  18.6 us (9%)
  between operations  16.3 us (8%)
  blocking collectives  13.3 us (6%)
  other arithmetic  6.92 us (3%)
    all_gather x1, waiting for transfers between devices, local(): gathered = lax.all_gather(token_rows, 'tensor', axis=0, tiled=True)  68.5 us
    dot_general x8, matrix products, local(): jnp.dot(onehot, values.reshape(entry_total, BH * BW), preferred_element_t...  46.7 us
    all_gather x1, waiting for transfers between devices, local(): lax.all_gather(outgoing, 'dp', axis=0, tiled=True)  27.6 us
    unnamed x1, blocking collectives  13.3 us
    dot_general x1, matrix products, local(): lax.dot_general(gathered, upstream, contract, preferred_element_type=jnp....  12.2 us
    unnamed x18, local copies, waits for them, and re-layouts  9.16 us
    reshape x1, local copies, waits for them, and re-layouts, to_blocks(): matrix.reshape(row_blocks, BH, col_blocks, BW).transpose(0, 2, 1, 3)  4.86 us
  transfers between devices with their start and end apart: 2, of which 2 were waited for; matrix products, arithmetic and copies ran while one was open for 1% of the time, Pallas kernels for 0%

commit v1 on v0

--- a/solution.py
+++ b/solution.py
@@ -37,7 +37,14 @@
     upstream = upstream_grad[0]
     shard_width = upstream.shape[1]
     contract = (((0,), (0,)), ((), ()))
-    gathered = lax.all_gather(token_rows, "tensor", axis=0, tiled=True)
+    ring = [token_rows]
+    for hop in range(3):
+        ring.append(lax.ppermute(ring[-1], "tensor", [(dev, (dev + 1) % 4) for dev in range(4)]))
+    gathered = jnp.roll(
+        jnp.concatenate(ring[::-1], axis=0),
+        (lax.axis_index("tensor") + 1) * ring[0].shape[0],
+        axis=0,
+    )
     gradient = lax.dot_general(gathered, upstream, contract, preferred_element_type=jnp.float32)
     accumulated = gradient + feedback[0].astype(jnp.float32)
     blocks = to_blocks(accumulated)

time: 211 us -> 270 us (1.28)
  waiting for transfers between devices: 96.8 us -> 131 us
  local copies, waits for them, and re-layouts: 18.6 us -> 38.1 us
  blocking collectives: 13.3 us -> 16.4 us
    ppermute x0 -> x3, waiting for transfers between devices: none -> 105 us  [local(): lax.ppermute(ring[-1], 'tensor', [(dev, (dev + 1) % 4) for dev in range(4)])]
    all_gather x1 -> x0, waiting for transfers between devices: 68.5 us -> none  [local(): gathered = lax.all_gather(token_rows, 'tensor', axis=0, tiled=True)]
    unnamed x18 -> x33, local copies, waits for them, and re-layouts: 9.16 us -> 27.3 us
    unnamed x1, blocking collectives: 13.3 us -> 16.4 us
  transfers between devices with their start and end apart: 2 -> 4, of which waited for: 2 -> 4; matrix products, arithmetic and copies ran while one was open for 1% -> 1% of each run, Pallas kernels for 0% -> 0%
where the time goes in v1:
time: 270 us; the launch traced here: 269 us
  waiting for transfers between devices  131 us (49%)
  matrix products  58.3 us (22%)
  local copies, waits for them, and re-layouts  38.1 us (14%)
  blocking collectives  16.4 us (6%)
  between operations  16.3 us (6%)
  other arithmetic  6.88 us (3%)
    ppermute x3, waiting for transfers between devices, local(): lax.ppermute(ring[-1], 'tensor', [(dev, (dev + 1) % 4) for dev in range(4)])  105 us
    dot_general x8, matrix products, local(): jnp.dot(onehot, values.reshape(entry_total, BH * BW), preferred_element_t...  46.8 us
    unnamed x33, local copies, waits for them, and re-layouts  27.3 us
    all_gather x1, waiting for transfers between devices, local(): lax.all_gather(outgoing, 'dp', axis=0, tiled=True)  25.3 us
    unnamed x1, blocking collectives  16.4 us
    dot_general x1, matrix products, local(): lax.dot_general(gathered, upstream, contract, preferred_element_type=jnp....  11.5 us
  transfers between devices with their start and end apart: 4, of which 4 were waited for; matrix products, arithmetic and copies ran while one was open for 1% of the time, Pallas kernels for 0%

profile of v1, /device:TPU:1, one launch (start us, length us, event | category | flops | bytes accessed | tf_op | source)
XLA Modules:
  0.0 269.2 jit_solution(6217930498317978492)
XLA Ops:
  7.2 2.5 collective-permute-start
  9.8 36.5 %collective-permute-done = bf16[384,2048]{1,0:T(8,128)(2,1)S(1)} collective-permute-done((bf16[384,2048]{1,0:T(8,128)(2,1)}, bf16[384,2048]{1,0:T(8,128)(2,1)S(1)}, u32[]{:S(2)}, u32[]{:S(2)}) %collective-permute-start) | collective-permute-done | bytes 1572896 | tf_op jit(solution)/shard_map/ppermute | solution.py:42
  46.2 1.1 copy-done.3
  47.4 36.0 %collective-permute-done.1 = bf16[384,2048]{1,0:T(8,128)(2,1)} collective-permute-done((bf16[384,2048]{1,0:T(8,128)(2,1)S(1)}, bf16[384,2048]{1,0:T(8,128)(2,1)}, u32[]{:S(2)}, u32[]{:S(2)}) %collective-permute-start.1) | collective-permute-done | bytes 1572896 | tf_op jit(solution)/shard_map/ppermute | solution.py:42
  83.3 0.7 compare_reduce_fusion
  84.2 0.8 fusion.44
  85.6 33.0 %collective-permute-done.2 = bf16[384,2048]{1,0:T(8,128)(2,1)} collective-permute-done((bf16[384,2048]{1,0:T(8,128)(2,1)}, bf16[384,2048]{1,0:T(8,128)(2,1)}, u32[]{:S(2)}, u32[]{:S(2)}) %collective-permute-start.2) | collective-permute-done | bytes 1572896 | tf_op jit(solution)/shard_map/ppermute | solution.py:42
  118.6 2.7 %constant_dynamic-update-slice_fusion.7 = bf16[3072,2048]{1,0:T(8,128)(2,1)} fusion(bf16[384,2048]{1,0:T(8,128)(2,1)} %collective-permute-done.2), kind=kLoop, calls=%fused_computation.65 | loop fusion | bytes 3145728
  121.3 2.8 %constant_dynamic-update-slice_fusion.6 = bf16[3072,2048]{1,0:T(8,128)(2,1)} fusion(bf16[3072,2048]{1,0:T(8,128)(2,1)} %constant_dynamic-update-slice_fusion.7, bf16[384,2048]{1,0:T(8,128)(2,1)} %collective-permute-done.1), kind=kLoop, calls=%fused_computation.64 | loop fusion | bytes 3145728
  124.2 2.7 %constant_dynamic-update-slice_fusion.5 = bf16[3072,2048]{1,0:T(8,128)(2,1)} fusion(bf16[3072,2048]{1,0:T(8,128)(2,1)} %constant_dynamic-update-slice_fusion.6, bf16[384,2048]{1,0:T(8,128)(2,1)} %copy-done.3), kind=kLoop, calls=%fused_computation.63 | loop fusion | bytes 3145728
  126.9 1.3 constant_dynamic-update-slice_fusion.4
  128.2 3.3 %constant_dynamic-update-slice_fusion.3 = bf16[3072,2048]{1,0:T(8,128)(2,1)} fusion(bf16[3072,2048]{1,0:T(8,128)(2,1)} %constant_dynamic-update-slice_fusion.4, bf16[384,2048]{1,0:T(8,128)(2,1)} %collective-permute-done.2), kind=kLoop, calls=%fused_computation.61 | loop fusion | bytes 3145728
  131.5 2.8 %constant_dynamic-update-slice_fusion.2 = bf16[3072,2048]{1,0:T(8,128)(2,1)} fusion(bf16[3072,2048]{1,0:T(8,128)(2,1)} %constant_dynamic-update-slice_fusion.3, bf16[384,2048]{1,0:T(8,128)(2,1)} %collective-permute-done.1), kind=kLoop, calls=%fused_computation.60 | loop fusion | bytes 3145728
  134.3 1.3 constant_dynamic-update-slice_fusion.1
  135.6 1.3 constant_dynamic-update-slice_fusion
  137.5 11.5 %fusion.3 = (bf16[1,2048,1024]{2,1,0:T(8,128)(2,1)}, f32[256,8,8,128]{3,1,2,0:T(8,128)S(1)}) fusion(pred[256,8,8,128]{3,2,1,0:T(8,128)(4,1)S(1)} %bitcast.149, bf16[1,2048,1024]{2,1,0:T(8,128)(2,1)S(1)} %copy-done.7, bf16[1,1536,1024]{2,1,0:T(8,128)(2,1)S(1)} %copy-done, bf16[3072,2048]{1,0:T(8,128)(2,1)} %constant_dynamic-update-slice_fusion, s32[]{:T(128)S(6)} %select_n.180), kind=kOutput, calls=%fused_computation.7 | convolution fusion | flops 6450839552 | bytes 28311556 | tf_op jit(solution)/shard_map/dot_general | solution.py:48
  149.0 2.1 copy.13
  151.2 4.9 %copy.12 = f32[32,64,8,128]{3,1,2,0:T(8,128)} copy(f32[32,64,8,128]{3,2,1,0:T(8,128)S(1)} %bitcast.136) | data formatting | bytes 16777216 | tf_op jit(solution)/shard_map/reshape | solution.py:19
  156.0 3.9 %gather_fusion = f32[2,64,128]{2,1,0:T(8,128)S(1)} fusion(f32[256,64,128]{2,1,0:T(8,128)} %bitcast.137, s32[1024]{0:T(1024)S(1)} %pad_clamp_fusion), kind=kCustom, calls=%fused_computation | custom fusion | bytes 131080 | tf_op jit(solution)/shard_map/gather | solution.py:55
  163.5 16.4 %all-reduce = s32[64]{0:T(128)S(1)} all-reduce(s32[64]{0:T(128)S(1)} %bitcast_dynamic-update-slice_fusion), channel_id=2, replica_groups=mesh['dp'=32,'tensor'=4] {'dp'}, use_global_device_ids=true, to_apply=%add | all-reduce | flops 64 | bytes 512
  180.0 25.3 %all-gather.3.cloned.1.call-done = bf16[64,64,128]{2,1,0:T(8,128)(2,1)} async-done(((bf16[2,64,128]{2,1,0:T(8,128)(2,1)}), bf16[64,64,128]{2,1,0:T(8,128)(2,1)}) %all-gather.3.cloned.1.call-update) | async-done | bytes 1048592 | tf_op jit(solution)/shard_map/all_gather | solution.py:60
  205.2 4.0 %bitcast_select_fusion = (bf16[64,64,128]{2,1,0:T(8,128)(2,1)S(1)}, bf16[64,64,128]{2,1,0:T(8,128)(2,1)S(1)}, bf16[64,64,128]{2,1,0:T(8,128)(2,1)S(1)}, bf16[64,...) fusion(bf16[64,64,128]{2,1,0:T(8,128)(2,1)} %all-gather.3.clone, ...), kind=kLoop, calls=%fused_computation.33 | loop fusion | flops 4194304 | bytes 17825800 | tf_op jit(solution)/shard_map/jit(_where)/select_n | solution.py:70
  209.2 1.3 fusion.7
  210.5 1.3 fusion.10
  211.8 4.5 %fusion.13 = f32[256,8192]{1,0:T(8,128)} fusion(bf16[8,8,64,128]{3,2,1,0:T(8,128)(2,1)S(1)} %bitcast.143, s32[64]{0:T(128)S(1)} %get-tuple-element.18), kind=kOutput, calls=%fused_computation.18 | convolution fusion | flops 268451840 | bytes 9437440 | tf_op jit(solution)/shard_map/dot_general | solution.py:73
  216.3 4.5 %fusion.16 = f32[256,8192]{1,0:T(8,128)} fusion(bf16[8,8,64,128]{3,2,1,0:T(8,128)(2,1)S(1)} %bitcast.142, s32[64]{0:T(128)S(1)} %get-tuple-element.17), kind=kOutput, calls=%fused_computation.21 | convolution fusion | flops 268451840 | bytes 9437440 | tf_op jit(solution)/shard_map/dot_general | solution.py:73
  220.8 4.5 %fusion.19 = f32[256,8192]{1,0:T(8,128)} fusion(bf16[8,8,64,128]{3,2,1,0:T(8,128)(2,1)S(1)} %bitcast.141, s32[64]{0:T(128)S(1)} %get-tuple-element.16), kind=kOutput, calls=%fused_computation.24 | convolution fusion | flops 268451840 | bytes 9437440 | tf_op jit(solution)/shard_map/dot_general | solution.py:73
  225.4 4.5 %fusion.22 = f32[256,8192]{1,0:T(8,128)} fusion(bf16[8,8,64,128]{3,2,1,0:T(8,128)(2,1)S(1)} %bitcast.140, s32[64]{0:T(128)S(1)} %get-tuple-element.15), kind=kOutput, calls=%fused_computation.27 | convolution fusion | flops 268451840 | bytes 9437440 | tf_op jit(solution)/shard_map/dot_general | solution.py:73
  229.9 4.5 %fusion.25 = f32[256,8192]{1,0:T(8,128)} fusion(bf16[8,8,64,128]{3,2,1,0:T(8,128)(2,1)S(1)} %bitcast.139, s32[64]{0:T(128)S(1)} %get-tuple-element.14), kind=kOutput, calls=%fused_computation.30 | convolution fusion | flops 268451840 | bytes 9437440 | tf_op jit(solution)/shard_map/dot_general | solution.py:73
  234.4 21.7 %divide_convert_fusion = bf16[256,8192]{1,0:T(8,128)(2,1)} fusion(f32[256,8192]{1,0:T(8,128)S(1)} %fusion.7, f32[256,8192]{1,0:T(8,128)S(1)} %fusion.10, f32[256,8192]{1,0:T(8,128)} %fusion.13, f32[256,8192]{1,0:T(8,128)} %fusion.16, f32[256,8192]{1,0:T(8,128)} %fusion.19, f32[256,8192]{1,0:T(8,128)} %fusion.22, f32[256,8192]{1,0:T(8,128)} %fusion.25, ...), kind=kOutput, calls=%fused_computation.3 | convolution fusion | flops 354435072 | bytes 63963456 | tf_op jit(solution)/shard_map/dot_general | solution.py:73
  256.0 5.4 %copy.60 = bf16[256,8,8,128]{3,1,2,0:T(8,128)(2,1)} copy(bf16[256,8,8,128]{3,2,1,0:T(8,128)(2,1)} %bitcast.147) | data formatting | bytes 8388608
  261.4 1.0 copy.71
  (32 shorter events, 2.9 us)
Async XLA Ops:
  7.2 130.3 %copy-start = (bf16[1,1536,1024]{2,1,0:T(8,128)(2,1)S(1)}, bf16[1,1536,1024]{2,1,0:T(8,128)(2,1)}, u32[]{:S(2)}) copy-start(bf16[1,1536,1024]{2,1,0:T(8,128)(2,1)} %param.8) | copy-start | bytes 9437188
  7.2 198.1 %all-gather.3.cloned.1.call-start = ((), (), s32[]{:S(2)}) async-start(), calls=%async_computation | async-start | bytes 1081344 | tf_op jit(solution)/shard_map/all_gather | solution.py:60
  7.2 39.0 %collective-permute-start = (bf16[384,2048]{1,0:T(8,128)(2,1)}, bf16[384,2048]{1,0:T(8,128)(2,1)S(1)}, u32[]{:S(2)}, u32[]{:S(2)}) collective-permute-start(bf16[384,2048]{1,0:T(8,128)(2,1)} %bitcast.138), channel_id=1, source_target_pairs={{0,1},{1,2},{2,3},{3,0},{4,5},{5,6},{6,7},{7,4},{8,9},{9,10},{10,1... | collective-permute-start | bytes 4718600 | tf_op jit(solution)/shard_map/ppermute | solution.py:42
  46.2 1.1 copy-start.3
  47.4 36.0 %collective-permute-start.1 = (bf16[384,2048]{1,0:T(8,128)(2,1)S(1)}, bf16[384,2048]{1,0:T(8,128)(2,1)}, u32[]{:S(2)}, u32[]{:S(2)}) collective-permute-start(bf16[384,2048]{1,0:T(8,128)(2,1)S(1)} %collective-permute-done), channel_id=1, source_target_pairs={{0,1},{1,2},{2,3},{3,0},{4,5},{5,6},{6,7},{7,4},{8,9},{9,10},{10,1... | collective-permute-start | bytes 4718600 | tf_op jit(solution)/shard_map/ppermute | solution.py:42
  83.3 35.3 %collective-permute-start.2 = (bf16[384,2048]{1,0:T(8,128)(2,1)}, bf16[384,2048]{1,0:T(8,128)(2,1)}, u32[]{:S(2)}, u32[]{:S(2)}) collective-permute-start(bf16[384,2048]{1,0:T(8,128)(2,1)} %collective-permute-done.1), channel_id=1, source_target_pairs={{0,1},{1,2},{2,3},{3,0},{4,5},{5,6},{6,7},{7,4},{8,9},{9,10},{10,1... | collective-permute-start | bytes 4718600 | tf_op jit(solution)/shard_map/ppermute | solution.py:42
  84.2 42.8 %copy-start.2 = (bf16[1,384,2048]{2,1,0:T(8,128)(2,1)S(1)}, bf16[1,384,2048]{2,1,0:T(8,128)(2,1)}, u32[]{:S(2)}) copy-start(bf16[1,384,2048]{2,1,0:T(8,128)(2,1)} %param.7) | copy-start | bytes 4718596
  121.3 13.0 %copy-start.4 = (bf16[384,2048]{1,0:T(8,128)(2,1)S(1)}, bf16[384,2048]{1,0:T(8,128)(2,1)}, u32[]{:S(2)}) copy-start(bf16[384,2048]{1,0:T(8,128)(2,1)} %copy-done.3) | copy-start | bytes 4718596
  126.9 10.6 %copy-start.7 = (bf16[1,2048,1024]{2,1,0:T(8,128)(2,1)S(1)}, bf16[1,2048,1024]{2,1,0:T(8,128)(2,1)}, u32[]{:S(2)}) copy-start(bf16[1,2048,1024]{2,1,0:T(8,128)(2,1)} %param.9) | copy-start | bytes 12582916
  151.1 11.0 %copy-start.9 = (u32[128]{0:T(128)S(1)}, u32[128]{0:T(128)}, u32[]{:S(2)}) copy-start(u32[128]{0:T(128)} %constant.117) | copy-start | bytes 1540
  151.1 12.3 %copy-start.8 = (s32[1,1,2]{2,1,0:T(1,128)S(1)}, s32[1,1,2]{2,1,0:T(1,128)}, u32[]{:S(2)}) copy-start(s32[1,1,2]{2,1,0:T(1,128)} %param.10) | copy-start | bytes 28
  151.2 28.8 %copy-start.6 = (s32[8,1,64]{2,1,0:T(1,128)S(1)}, s32[8,1,64]{2,1,0:T(1,128)}, u32[]{:S(2)}) copy-start(s32[8,1,64]{2,1,0:T(1,128)} %param.12) | copy-start | bytes 6148
  234.4 28.0 %copy-start.1 = (bf16[1,1536,1024]{2,1,0:T(8,128)(2,1)S(1)}, bf16[1,1536,1024]{2,1,0:T(8,128)(2,1)}, u32[]{:S(2)}) copy-start(bf16[1,1536,1024]{2,1,0:T(8,128)(2,1)} %param.8) | copy-start | bytes 9437188
  256.0 5.4 %copy-start.5 = (bf16[64,64,128]{2,1,0:T(8,128)(2,1)S(1)}, bf16[64,64,128]{2,1,0:T(8,128)(2,1)}, u32[]{:S(2)}) copy-start(bf16[64,64,128]{2,1,0:T(8,128)(2,1)} %all-gather.3.cloned.1.call-done) | copy-start | bytes 3145732
Sparse Core Ops, SparseCore 0:
  160.8 44.3 all-gather.2
